TPU v7x, 32 devices: a whole 2x2x4 slice. The times are simulated.
32 devices in a mesh: slab: 2 (over x), line: 8 (over z, y), band: 2 (over core).
Axes of the slice: x: 2, y: 2, z: 4, core: 2. Of those that a mesh axis runs over, the one named last changes fastest.
Arguments:
- cube: bfloat16 [230, 2048, 256], P('band', ('slab', 'line')), parts along dimension 1, may hold values from -6 to 6
- observed: bfloat16 [13, 2048, 256], P(None, ('slab', 'line')), parts along dimension 1, may hold values from -6 to 6
- along_kernels: bfloat16 [3, 128, 128], replicated, may hold values from -0.3125 to 0.3125
- along_offsets: int32 [3], replicated, may hold values from -1 to 1, as said below
- across_kernels: bfloat16 [3, 128, 128], replicated, may hold values from -0.3125 to 0.3125
- across_offsets: int32 [3], replicated, may hold values from -1 to 1, as said below
- resp_start: int32 [13], replicated, may hold values from 0 to 21
- resp_values: bfloat16 [13, 20], replicated, may hold values from 0.049804688 to 0.3984375
Outputs:
- synthetic: float32 [13, 2048, 256], P(None, ('slab', 'line')), parts along dimension 1
- angles: float32 [2048, 256], P(('slab', 'line')), parts along dimension 0
There are 2 independent parts, one for each index of `slab`. A program takes and returns all parts, laid end to end along the dimension named above; an argument that names none is the same for every part. Nothing has to cross between parts.
Inputs may be any that keep to these rules, and one draw needn't show every extreme that they name: `along_offsets`: the three entries are -1, 0 and 1, each once. `across_offsets`: the three entries are -1, 0 and 1, each once.
All inputs are finite; a program needn't handle non-finite values.
Results may differ from a plain program's by a relative error of at most 0.0003.
Values may be sent and summed in bfloat16 or wider, within the bound.
A program may use at most 192 MiB of HBM per device.

v0:
```python
import jax
import jax.numpy as jnp
from jax import lax
from jax.sharding import PartitionSpec as P

BLK = 128
SPB = 10


def extended(shard, sides, width):
    for axis, dim in sides:
        size, length = (lax.axis_size(axis), shard.shape[dim])
        up = [(i, (i + 1) % size) for i in range(size - 1)]
        down = [(j, i) for i, j in up]
        last = lax.slice_in_dim(shard, length - width, length, axis=dim)
        leading = lax.slice_in_dim(shard, 0, width, axis=dim)
        before = lax.ppermute(last, axis, up)
        after = lax.ppermute(leading, axis, down)
        shard = jnp.concatenate([before, shard, after], axis=dim)
    return shard


def pick_kernels(kernels, offsets):
    shifts = jnp.arange(3, dtype=jnp.int32) - 1
    onehot = (offsets[None, :] == shifts[:, None]).astype(jnp.float32)
    return jnp.einsum(
        "sk,kpq->spq", onehot, kernels.astype(jnp.float32), precision=lax.Precision.HIGHEST
    )


def dense_response(resp_start, resp_values, band_total):
    bands = jnp.arange(band_total, dtype=jnp.int32)
    local = bands[None, :] - SPB * resp_start[:, None]
    slots = jnp.arange(2 * SPB, dtype=jnp.int32)
    hits = local[:, :, None] == slots[None, None, :]
    return jnp.sum(
        jnp.where(hits, resp_values.astype(jnp.float32)[:, None, :], jnp.float32(0.0)), axis=-1
    )


def along_blocks(padded, chosen, count):
    total = None
    for index in range(3):
        term = jnp.einsum(
            "pq,bnqc->bnpc",
            chosen[index],
            padded[:, index : index + count],
            precision=lax.Precision.HIGHEST,
        )
        total = term if total is None else total + term
    return total


def across_filter(field, chosen):
    count = field.shape[2] // BLK
    blocks = field.reshape(field.shape[0], field.shape[1], count, BLK)
    padded = jnp.pad(blocks, ((0, 0), (0, 0), (1, 1), (0, 0)))
    total = jnp.zeros(blocks.shape, jnp.float32)
    for index in range(3):
        total = total + jnp.einsum(
            "pq,blnq->blnp",
            chosen[index],
            padded[:, :, index : index + count],
            precision=lax.Precision.HIGHEST,
        )
    return total.reshape(field.shape)


def respond_plain(weights, field):
    return jnp.einsum(
        "mb,blc->mlc", weights.astype(jnp.bfloat16), field, preferred_element_type=jnp.float32
    )


def on_device(
    cube,
    observed,
    along_kernels,
    along_offsets,
    across_kernels,
    across_offsets,
    resp_start,
    resp_values,
):
    band_share = cube.shape[0]
    line_rows = cube.shape[1]
    column_count = cube.shape[2]
    band_total = band_share * lax.axis_size("band")
    along_pick = pick_kernels(along_kernels, along_offsets)
    across_pick = pick_kernels(across_kernels, across_offsets)
    response = dense_response(resp_start, resp_values, band_total)
    local_response = lax.dynamic_slice_in_dim(
        response, lax.axis_index("band") * band_share, band_share, 1
    )
    count = line_rows // BLK
    folded = respond_plain(local_response, cube)
    summed = lax.psum(folded, "band")
    padded_sum = extended(summed, (("line", 1),), BLK)
    padded = padded_sum.reshape(summed.shape[0], count + 2, BLK, column_count)
    smooth = along_blocks(padded, along_pick, count).reshape(summed.shape)
    partial_value = across_filter(smooth, across_pick)
    seen = observed.astype(jnp.float32)
    inner = jnp.sum(partial_value * seen, axis=0)
    first = jnp.sqrt(jnp.sum(partial_value * partial_value, axis=0))
    second = jnp.sqrt(jnp.sum(seen * seen, axis=0))
    angles = jnp.arccos(jnp.clip(inner / jnp.maximum(first * second, 1.0), -1.0, 1.0))
    return (partial_value, angles)


def solution(mesh):
    placed = (
        P("band", ("slab", "line"), None),
        P(None, ("slab", "line"), None),
        P(),
        P(),
        P(),
        P(),
        P(),
        P(),
    )
    return jax.shard_map(
        on_device,
        mesh=mesh,
        in_specs=placed,
        out_specs=(P(None, ("slab", "line"), None), P(("slab", "line"), None)),
        check_vma=False,
    )
```

profile of v0, /device:TPU:0, one launch (start us, length us, event | category | flops | bytes accessed | tf_op | source)
XLA Modules:
  0.0 157.4 jit_solution(8674825454620172075)
XLA Ops:
  8.8 8.8 %fusion = f32[13,128,256]{2,0,1:T(8,128)} fusion(bf16[115,128,256]{2,1,0:T(8,128)(2,1)} %param.8, bf16[13,230]{1,0:T(8,128)(2,1)S(1)} %select_reduce_fusion, s32[]{:T(128)S(6)} %select_n.8), kind=kOutput, calls=%fused_computation | convolution fusion | flops 97976320 | bytes 9244676 | tf_op jit(solution)/shard_map/mb,blc->mlc/dot_general | solution.py:70
  17.6 24.1 %all-reduce.3.cloned.1.call-done = f32[13,128,256]{2,0,1:T(8,128)} async-done(((f32[13,128,256]{2,0,1:T(8,128)}), f32[13,128,256]{2,0,1:T(8,128)}) %all-reduce.3.cloned.1.call-update) | async-done | bytes 1703952 | tf_op jit(solution)/shard_map/psum | solution.py:97
  41.8 2.6 %copy.36 = f32[13,128,256]{2,1,0:T(8,128)S(1)} copy(f32[13,128,256]{2,0,1:T(8,128)} %all-reduce.3.cloned.1.call-done) | data formatting | bytes 3407872 | tf_op jit(solution)/shard_map/psum | solution.py:97
  44.4 3.8 %collective-permute-start = (f32[13,128,256]{2,1,0:T(8,128)S(1)}, f32[13,128,256]{2,1,0:T(8,128)S(1)}, u32[]{:S(2)}, u32[]{:S(2)}) collective-permute-start(f32[13,128,256]{2,1,0:T(8,128)S(1)} %copy.36), channel_id=1, source_target_pairs={{0,2},{2,4},{4,6},{6,8},{8,10},{10,12},{12,14},{1,3},{3,5},{5,7},{... | collective-permute-start | bytes 5111816 | tf_op jit(solution)/shard_map/ppermute | solution.py:17
  48.1 1.3 collective-permute-start.1
  50.2 0.8 fusion.28
  50.9 70.5 %collective-permute-done = f32[13,128,256]{2,1,0:T(8,128)S(1)} collective-permute-done((f32[13,128,256]{2,1,0:T(8,128)S(1)}, f32[13,128,256]{2,1,0:T(8,128)S(1)}, u32[]{:S(2)}, u32[]{:S(2)}) %collective-permute-start) | collective-permute-done | bytes 1703968 | tf_op jit(solution)/shard_map/ppermute | solution.py:17
  121.4 1.0 copy.38
  122.5 1.0 copy.39
  124.0 0.7 pad_maximum_fusion
  124.8 2.6 %fusion.27 = (f32[13,1,128,256]{3,0,2,1:T(8,128)S(1)}, f32[13,1,128,256]{3,0,2,1:T(8,128)}, f32[13,1,128,256]{3,0,2,1:T(8,128)}) fusion(f32[13,3,128,256]{3,0,2,1:T(8,128)S(1)} %bitcast.67), kind=kLoop, calls=%fused_computation.37 | loop fusion | bytes 10223616 | tf_op jit(solution)/shard_map/slice | solution.py:47
  127.4 2.9 %copy.55 = f32[13,1,128,256]{2,3,0,1:T(8,128)} copy(f32[13,1,128,256]{3,0,2,1:T(8,128)} %get-tuple-element.11) | data formatting | bytes 3407872
  130.3 2.8 %copy.56 = f32[13,1,128,256]{2,3,0,1:T(8,128)} copy(f32[13,1,128,256]{3,0,2,1:T(8,128)} %get-tuple-element.12) | data formatting | bytes 3407872
  133.1 1.8 %copy.54 = f32[13,1,128,256]{2,3,0,1:T(8,128)} copy(f32[13,1,128,256]{3,0,2,1:T(8,128)S(1)} %get-tuple-element.10) | data formatting | bytes 3407872
  134.8 3.1 %fusion.6 = f32[13,256,128]{2,1,0:T(8,128)S(1)} fusion(f32[128,128,1]{1,0,2:T(8,128)S(1)} %bitcast.75, f32[13,1,128,256]{2,3,0,1:T(8,128)} %copy.55), kind=kOutput, calls=%fused_computation.9 | convolution fusion | flops 654311424 | bytes 3473408 | tf_op jit(solution)/shard_map/pq,bnqc->bnpc/dot_general | solution.py:44
  138.0 1.6 %fusion.4 = f32[13,256,128]{2,1,0:T(8,128)S(1)} fusion(f32[128,128,1]{1,0,2:T(8,128)S(1)} %bitcast.74, f32[13,1,128,256]{2,3,0,1:T(8,128)S(1)} %copy-done.3), kind=kOutput, calls=%fused_computation.7 | convolution fusion | flops 654311424 | bytes 3473408 | tf_op jit(solution)/shard_map/pq,bnqc->bnpc/dot_general | solution.py:44
  139.6 1.6 %add_add_fusion.1 = f32[13,256,128]{2,1,0:T(8,128)S(1)} fusion(f32[13,256,128]{2,1,0:T(8,128)S(1)} %fusion.4, f32[13,256,128]{2,1,0:T(8,128)S(1)} %fusion.6, f32[128,128,1]{1,0,2:T(8,128)S(1)} %bitcast.71, f32[13,1,128,256]{2,3,0,1:T(8,128)S(1)} %copy-done.4), kind=kOutput, calls=%fused_computation.15 | convolution fusion | flops 655163392 | bytes 6881280 | tf_op jit(solution)/shard_map/pq,bnqc->bnpc/dot_general | solution.py:44
  141.2 1.6 %fusion.30 = f32[13,128,2,128]{1,3,2,0:T(8,128)S(1)} fusion(f32[13,128,2,128]{1,3,2,0:T(8,128)S(1)} %bitcast.64, f32[128,128,1,1]{1,0,3,2:T(8,128)S(1)} %bitcast.73), kind=kOutput, calls=%fused_computation.40 | convolution fusion | flops 654311424 | bytes 3473408 | tf_op jit(solution)/shard_map/pq,blnq->blnp/dot_general | solution.py:60
  142.9 1.5 fusion.31
  144.4 1.8 %multiply_reduce_fusion = (f32[128,2,128]{0,2,1:T(8,128)}, f32[13,128,2,128]{1,3,2,0:T(8,128)S(1)}) fusion(f32[13,128,2,128]{1,3,2,0:T(8,128)S(1)} %bitcast.66, f32[128,128,1,1]{1,0,3,2:T(8,128)S(1)} %bitcast.70, f32[13,128,2,128]{1,3,2,0:T(8,128)S(1)} %fusion.31, f32[13,128,2,128]{1,3,2,0:T(8,128)S(1)} %fusion.30), kind=kOutput, calls=%fused_computation.13 | convolution fusion | flops 328826880 | bytes 7012352 | tf_op jit(solution)/shard_map/pq,blnq->blnp/dot_general | solution.py:60
  146.1 0.7 copy.49
  146.9 1.1 sqrt.9
  148.1 1.5 fusion.3
  149.5 1.0 sqrt_atan2_fusion
  (30 shorter events, 3.0 us)
Async XLA Ops:
  7.2 42.3 %copy-start = (bf16[3,128,128]{2,1,0:T(8,128)(2,1)S(1)}, bf16[3,128,128]{2,1,0:T(8,128)(2,1)}, u32[]{:S(2)}) copy-start(bf16[3,128,128]{2,1,0:T(8,128)(2,1)} %param.10) | copy-start | bytes 294916
  7.2 34.6 %all-reduce.3.cloned.1.call-start = ((), (), s32[]{:S(2)}) async-start(), calls=%async_computation | async-start | bytes 4194304 | tf_op jit(solution)/shard_map/psum | solution.py:97
  17.6 31.8 %copy-start.7 = (s32[3]{0:T(128)S(1)}, s32[3]{0:T(128)}, u32[]{:S(2)}) copy-start(s32[3]{0:T(128)} %param.11) | copy-start | bytes 40
  17.6 32.1 %copy-start.6 = (bf16[3,128,128]{2,1,0:T(8,128)(2,1)S(1)}, bf16[3,128,128]{2,1,0:T(8,128)(2,1)}, u32[]{:S(2)}) copy-start(bf16[3,128,128]{2,1,0:T(8,128)(2,1)} %param.12) | copy-start | bytes 294916
  17.6 32.1 %copy-start.8 = (s32[3]{0:T(128)S(1)}, s32[3]{0:T(128)}, u32[]{:S(2)}) copy-start(s32[3]{0:T(128)} %param.13) | copy-start | bytes 40
  44.4 77.1 %collective-permute-start = (f32[13,128,256]{2,1,0:T(8,128)S(1)}, f32[13,128,256]{2,1,0:T(8,128)S(1)}, u32[]{:S(2)}, u32[]{:S(2)}) collective-permute-start(f32[13,128,256]{2,1,0:T(8,128)S(1)} %copy.36), channel_id=1, source_target_pairs={{0,2},{2,4},{4,6},{6,8},{8,10},{10,12},{12,14},{1,3},{3,5},{5,7},{... | collective-permute-start | bytes 5111816 | tf_op jit(solution)/shard_map/ppermute | solution.py:17
  48.1 74.3 %collective-permute-start.1 = (f32[13,128,256]{2,1,0:T(8,128)S(1)}, f32[13,128,256]{2,1,0:T(8,128)S(1)}, u32[]{:S(2)}, u32[]{:S(2)}) collective-permute-start(f32[13,128,256]{2,1,0:T(8,128)S(1)} %copy.36), channel_id=1, source_target_pairs={{2,0},{4,2},{6,4},{8,6},{10,8},{12,10},{14,12},{3,1},{5,3},{7,5},{... | collective-permute-start | bytes 5111816 | tf_op jit(solution)/shard_map/ppermute | solution.py:18
  122.4 1.6 %copy-start.1 = (f32[13,128,256]{2,0,1:T(8,128)S(1)}, f32[13,128,256]{2,0,1:T(8,128)}, u32[]{:S(2)}) copy-start(f32[13,128,256]{2,0,1:T(8,128)} %all-reduce.3.cloned.1.call-done) | copy-start | bytes 5111812
  134.8 3.1 %copy-start.3 = (f32[13,1,128,256]{2,3,0,1:T(8,128)S(1)}, f32[13,1,128,256]{2,3,0,1:T(8,128)}, u32[]{:S(2)}) copy-start(f32[13,1,128,256]{2,3,0,1:T(8,128)} %copy.56) | copy-start | bytes 5111812
  138.0 1.6 %copy-start.4 = (f32[13,1,128,256]{2,3,0,1:T(8,128)S(1)}, f32[13,1,128,256]{2,3,0,1:T(8,128)}, u32[]{:S(2)}) copy-start(f32[13,1,128,256]{2,3,0,1:T(8,128)} %copy.54) | copy-start | bytes 5111812
  142.8 1.5 copy-start.5
  146.9 3.6 %copy-start.2 = (f32[13,128,256]{2,1,0:T(8,128)}, f32[13,128,256]{2,1,0:T(8,128)S(1)}, u32[]{:S(2)}) copy-start(f32[13,128,256]{2,1,0:T(8,128)S(1)} %copy.49) | copy-start | bytes 5111812
Sparse Core Ops, SparseCore 0:
  17.7 24.0 all-reduce.2
where the time goes:
time: 158 us; the launch traced here: 157 us
  waiting for transfers between devices  94.6 us (60%)
  matrix products  20.5 us (13%)
  local copies, waits for them, and re-layouts  18.1 us (11%)
  between operations  14.3 us (9%)
  starting transfers between devices  5.09 us (3%)
  other arithmetic  4.75 us (3%)
    ppermute x1, waiting for transfers between devices, extended(): before = lax.ppermute(last, axis, up)  70.5 us
    psum x1, waiting for transfers between devices, on_device(): summed = lax.psum(folded, 'band')  24.1 us
    dot_general x1, matrix products, respond_plain(): jnp.einsum('mb,blc->mlc', weights.astype(jnp.bfloat16), field, preferred_...  8.77 us
    unnamed x22, local copies, waits for them, and re-layouts  8.75 us
    dot_general x3, matrix products, along_blocks(): jnp.einsum('pq,bnqc->bnpc', chosen[index], padded[:, index:index + count]...  6.31 us
    dot_general x3, matrix products, across_filter(): jnp.einsum('pq,blnq->blnp', chosen[index], padded[:, :, index:index + cou...  4.89 us
    ppermute x1, starting transfers between devices, extended(): before = lax.ppermute(last, axis, up)  3.76 us
  transfers between devices with their start and end apart: 3, of which 2 were waited for; matrix products, arithmetic and copies ran while one was open for 2% of the time, Pallas kernels for 0%

commit v1 on v0

--- a/solution.py
+++ b/solution.py
@@ -94,7 +94,7 @@
     )
     count = line_rows // BLK
     folded = respond_plain(local_response, cube)
-    summed = lax.psum(folded, "band")
+    summed = jnp.sum(lax.all_gather(folded, "band"), axis=0)
     padded_sum = extended(summed, (("line", 1),), BLK)
     padded = padded_sum.reshape(summed.shape[0], count + 2, BLK, column_count)
     smooth = along_blocks(padded, along_pick, count).reshape(summed.shape)

time: 158 us -> 140 us (0.89)
  local copies, waits for them, and re-layouts: 18.1 us -> 4.4 us
  waiting for transfers between devices: 94.6 us -> 86.3 us
  other arithmetic: 4.75 us -> 6.76 us
    psum x1 -> x0, waiting for transfers between devices: 24.1 us -> none  [on_device(): summed = lax.psum(folded, 'band')]
    all_gather x0 -> x1, waiting for transfers between devices: none -> 15.4 us  [on_device(): summed = jnp.sum(lax.all_gather(folded, 'band'), axis=0)]
    unnamed x22 -> x11, local copies, waits for them, and re-layouts: 8.75 us -> 0.77 us
    slice x1 -> x0, local copies, waits for them, and re-layouts: 2.65 us -> none  [along_blocks(): padded[:, index:index + count]]
    psum x1 -> x0, local copies, waits for them, and re-layouts: 2.58 us -> none  [on_device(): summed = lax.psum(folded, 'band')]
    reduce_sum x0 -> x1, other arithmetic: none -> 2.4 us  [on_device(): summed = jnp.sum(lax.all_gather(folded, 'band'), axis=0)]
    dot_general x3, matrix products: 6.31 us -> 8.65 us  [along_blocks(): jnp.einsum('pq,bnqc->bnpc', chosen[index], padded[:, index:index + count]...]
    dot_general x0 -> x1, local copies, waits for them, and re-layouts: none -> 2.18 us  [respond_plain(): jnp.einsum('mb,blc->mlc', weights.astype(jnp.bfloat16), field, preferred_...]
  transfers between devices with their start and end apart: 3 -> 3, of which waited for: 2 -> 2; matrix products, arithmetic and copies ran while one was open for 2% -> 1% of each run, Pallas kernels for 0% -> 0%
where the time goes in v1:
time: 140 us; the launch traced here: 139 us
  waiting for transfers between devices  86.3 us (62%)
  matrix products  21.8 us (16%)
  between operations  14.2 us (10%)
  other arithmetic  6.76 us (5%)
  starting transfers between devices  5.27 us (4%)
  local copies, waits for them, and re-layouts  4.4 us (3%)
    ppermute x1, waiting for transfers between devices, extended(): before = lax.ppermute(last, axis, up)  70.9 us
    all_gather x1, waiting for transfers between devices, on_device(): summed = jnp.sum(lax.all_gather(folded, 'band'), axis=0)  15.4 us
    dot_general x3, matrix products, along_blocks(): jnp.einsum('pq,bnqc->bnpc', chosen[index], padded[:, index:index + count]...  8.65 us
    dot_general x1, matrix products, respond_plain(): jnp.einsum('mb,blc->mlc', weights.astype(jnp.bfloat16), field, preferred_...  7.46 us
    dot_general x3, matrix products, across_filter(): jnp.einsum('pq,blnq->blnp', chosen[index], padded[:, :, index:index + cou...  5.13 us
    ppermute x1, starting transfers between devices, extended(): before = lax.ppermute(last, axis, up)  3.75 us
  transfers between devices with their start and end apart: 3, of which 2 were waited for; matrix products, arithmetic and copies ran while one was open for 1% of the time, Pallas kernels for 0%

profile of v1, /device:TPU:0, one launch (start us, length us, event | category | flops | bytes accessed | tf_op | source)
XLA Modules:
  0.0 138.8 jit_solution(430036859707887252)
XLA Ops:
  7.2 0.7 broadcast_multiply_fusion
  8.0 0.7 convert_element_type.8
  8.7 0.1 select_reduce_fusion
  8.8 7.5 %fusion = f32[13,128,256]{2,0,1:T(8,128)S(1)} fusion(bf16[115,128,256]{2,1,0:T(8,128)(2,1)} %param.8, bf16[13,230]{1,0:T(8,128)(2,1)S(1)} %select_reduce_fusion, s32[]{:T(128)S(6)} %select_n.8), kind=kOutput, calls=%fused_computation | convolution fusion | flops 97976320 | bytes 9244676 | tf_op jit(solution)/shard_map/mb,blc->mlc/dot_general | solution.py:70
  16.3 2.2 %copy.41 = f32[13,128,256]{2,1,0:T(8,128)} copy(f32[13,128,256]{2,0,1:T(8,128)S(1)} %fusion) | data formatting | bytes 3407872 | tf_op jit(solution)/shard_map/mb,blc->mlc/dot_general | solution.py:70
  18.5 15.4 %all-gather.3.cloned.1.call-done = f32[26,128,256]{2,1,0:T(8,128)} async-done(((f32[13,128,256]{2,1,0:T(8,128)}), f32[26,128,256]{2,1,0:T(8,128)}) %all-gather.3.cloned.1.call-update) | async-done | bytes 3407888 | tf_op jit(solution)/shard_map/all_gather | solution.py:97
  33.9 2.4 %reduce_sum.46 = f32[13,128,256]{2,1,0:T(8,128)S(1)} reduce(f32[2,13,128,256]{3,2,1,0:T(8,128)} %bitcast.75, f32[]{:T(128)} %constant.10.clone.1), dimensions={0}, to_apply=%region_1.2 | reduce | flops 425984 | bytes 5111812 | tf_op jit(solution)/shard_map/reduce_sum | solution.py:97
  36.3 3.8 %collective-permute-start = (f32[13,128,256]{2,1,0:T(8,128)S(1)}, f32[13,128,256]{2,1,0:T(8,128)S(1)}, u32[]{:S(2)}, u32[]{:S(2)}) collective-permute-start(f32[13,128,256]{2,1,0:T(8,128)S(1)} %reduce_sum.46), channel_id=1, source_target_pairs={{0,2},{2,4},{4,6},{6,8},{8,10},{10,12},{12,14},{1,3},{3,5},{5,7},{... | collective-permute-start | bytes 5111816 | tf_op jit(solution)/shard_map/ppermute | solution.py:17
  40.0 1.5 %collective-permute-start.1 = (f32[13,128,256]{2,1,0:T(8,128)S(1)}, f32[13,128,256]{2,1,0:T(8,128)S(1)}, u32[]{:S(2)}, u32[]{:S(2)}) collective-permute-start(f32[13,128,256]{2,1,0:T(8,128)S(1)} %reduce_sum.46), channel_id=1, source_target_pairs={{2,0},{4,2},{6,4},{8,6},{10,8},{12,10},{14,12},{3,1},{5,3},{7,5},{... | collective-permute-start | bytes 5111816 | tf_op jit(solution)/shard_map/ppermute | solution.py:18
  41.5 0.3 fusion.9
  41.8 0.3 fusion.7
  42.1 0.1 fusion.23
  42.4 70.9 %collective-permute-done = f32[13,128,256]{2,1,0:T(8,128)S(1)} collective-permute-done((f32[13,128,256]{2,1,0:T(8,128)S(1)}, f32[13,128,256]{2,1,0:T(8,128)S(1)}, u32[]{:S(2)}, u32[]{:S(2)}) %collective-permute-start) | collective-permute-done | bytes 1703968 | tf_op jit(solution)/shard_map/ppermute | solution.py:17
  113.3 0.3 pad_maximum_fusion
  113.7 2.9 %fusion.5 = f32[13,256,128]{2,1,0:T(8,128)S(1)} fusion(f32[128,128,1]{1,0,2:T(8,128)S(1)} %bitcast.82, f32[13,3,128,256]{3,2,1,0:T(8,128)S(1)} %bitcast.71), kind=kOutput, calls=%fused_computation.10 | convolution fusion | flops 654311424 | bytes 3473408 | tf_op jit(solution)/shard_map/pq,bnqc->bnpc/dot_general | solution.py:44
  116.6 2.9 %fusion.6 = f32[13,256,128]{2,1,0:T(8,128)S(1)} fusion(f32[128,128,1]{1,0,2:T(8,128)S(1)} %bitcast.81, f32[13,3,128,256]{3,2,1,0:T(8,128)S(1)} %bitcast.72), kind=kOutput, calls=%fused_computation.12 | convolution fusion | flops 654311424 | bytes 3473408 | tf_op jit(solution)/shard_map/pq,bnqc->bnpc/dot_general | solution.py:44
  119.5 2.9 %add_add_fusion.1 = f32[13,256,128]{2,1,0:T(8,128)S(1)} fusion(f32[13,256,128]{2,1,0:T(8,128)S(1)} %fusion.6, f32[13,256,128]{2,1,0:T(8,128)S(1)} %fusion.5, f32[128,128,1]{1,0,2:T(8,128)S(1)} %bitcast.78, f32[13,3,128,256]{3,2,1,0:T(8,128)S(1)} %bitcast.73), kind=kOutput, calls=%fused_computation.15 | convolution fusion | flops 655163392 | bytes 6881280 | tf_op jit(solution)/shard_map/pq,bnqc->bnpc/dot_general | solution.py:44
  122.4 1.6 %fusion.24 = f32[13,128,2,128]{1,3,2,0:T(8,128)S(1)} fusion(f32[13,128,2,128]{1,3,2,0:T(8,128)S(1)} %bitcast.68, f32[128,128,1,1]{1,0,3,2:T(8,128)S(1)} %bitcast.80), kind=kOutput, calls=%fused_computation.39 | convolution fusion | flops 654311424 | bytes 3473408 | tf_op jit(solution)/shard_map/pq,blnq->blnp/dot_general | solution.py:60
  124.0 1.7 %fusion.25 = f32[13,128,2,128]{1,3,2,0:T(8,128)S(1)} fusion(f32[13,128,2,128]{1,3,2,0:T(8,128)S(1)} %bitcast.69, f32[128,128,1,1]{1,0,3,2:T(8,128)S(1)} %bitcast.79), kind=kOutput, calls=%fused_computation.40 | convolution fusion | flops 327155712 | bytes 3473408 | tf_op jit(solution)/shard_map/pq,blnq->blnp/dot_general | solution.py:60
  125.7 1.8 %multiply_reduce_fusion = (f32[128,2,128]{0,2,1:T(8,128)}, f32[13,128,2,128]{1,3,2,0:T(8,128)S(1)}) fusion(f32[13,128,2,128]{1,3,2,0:T(8,128)S(1)} %bitcast.70, f32[128,128,1,1]{1,0,3,2:T(8,128)S(1)} %bitcast.77, f32[13,128,2,128]{1,3,2,0:T(8,128)S(1)} %fusion.25, f32[13,128,2,128]{1,3,2,0:T(8,128)S(1)} %fusion.24), kind=kOutput, calls=%fused_computation.13 | convolution fusion | flops 328826880 | bytes 7012352 | tf_op jit(solution)/shard_map/pq,blnq->blnp/dot_general | solution.py:60
  127.5 0.7 copy.51
  128.3 1.1 sqrt.9
  129.5 1.5 %fusion.3 = (f32[128,256]{1,0:T(8,128)S(1)}, f32[128,256]{1,0:T(8,128)S(1)}) fusion(bf16[13,128,256]{2,1,0:T(8,128)(2,1)} %param.9, f32[13,128,256]{2,1,0:T(8,128)S(1)} %copy.51), kind=kLoop, calls=%fused_computation.6 | loop fusion | flops 2064384 | bytes 2818048 | tf_op jit(solution)/shard_map/reduce_sum | solution.py:105
  130.9 1.0 sqrt_atan2_fusion
  (17 shorter events, 0.4 us)
Async XLA Ops:
  7.2 34.4 %copy-start = (bf16[3,128,128]{2,1,0:T(8,128)(2,1)S(1)}, bf16[3,128,128]{2,1,0:T(8,128)(2,1)}, u32[]{:S(2)}) copy-start(bf16[3,128,128]{2,1,0:T(8,128)(2,1)} %param.10) | copy-start | bytes 294916
  7.2 26.7 %all-gather.3.cloned.1.call-start = ((), (), s32[]{:S(2)}) async-start(), calls=%async_computation | async-start | bytes 5111808 | tf_op jit(solution)/shard_map/all_gather | solution.py:97
  33.9 7.7 %copy-start.3 = (s32[3]{0:T(128)S(1)}, s32[3]{0:T(128)}, u32[]{:S(2)}) copy-start(s32[3]{0:T(128)} %param.11) | copy-start | bytes 40
  33.9 8.0 %copy-start.2 = (bf16[3,128,128]{2,1,0:T(8,128)(2,1)S(1)}, bf16[3,128,128]{2,1,0:T(8,128)(2,1)}, u32[]{:S(2)}) copy-start(bf16[3,128,128]{2,1,0:T(8,128)(2,1)} %param.12) | copy-start | bytes 294916
  33.9 8.0 %copy-start.4 = (s32[3]{0:T(128)S(1)}, s32[3]{0:T(128)}, u32[]{:S(2)}) copy-start(s32[3]{0:T(128)} %param.13) | copy-start | bytes 40
  36.3 77.1 %collective-permute-start = (f32[13,128,256]{2,1,0:T(8,128)S(1)}, f32[13,128,256]{2,1,0:T(8,128)S(1)}, u32[]{:S(2)}, u32[]{:S(2)}) collective-permute-start(f32[13,128,256]{2,1,0:T(8,128)S(1)} %reduce_sum.46), channel_id=1, source_target_pairs={{0,2},{2,4},{4,6},{6,8},{8,10},{10,12},{12,14},{1,3},{3,5},{5,7},{... | collective-permute-start | bytes 5111816 | tf_op jit(solution)/shard_map/ppermute | solution.py:17
  40.0 73.3 %collective-permute-start.1 = (f32[13,128,256]{2,1,0:T(8,128)S(1)}, f32[13,128,256]{2,1,0:T(8,128)S(1)}, u32[]{:S(2)}, u32[]{:S(2)}) collective-permute-start(f32[13,128,256]{2,1,0:T(8,128)S(1)} %reduce_sum.46), channel_id=1, source_target_pairs={{2,0},{4,2},{6,4},{8,6},{10,8},{12,10},{14,12},{3,1},{5,3},{7,5},{... | collective-permute-start | bytes 5111816 | tf_op jit(solution)/shard_map/ppermute | solution.py:18
  128.3 3.6 %copy-start.1 = (f32[13,128,256]{2,1,0:T(8,128)}, f32[13,128,256]{2,1,0:T(8,128)S(1)}, u32[]{:S(2)}) copy-start(f32[13,128,256]{2,1,0:T(8,128)S(1)} %copy.51) | copy-start | bytes 5111812
Sparse Core Ops, SparseCore 0:
  18.6 15.2 all-gather.2
